TPU v7x, 32 devices: a whole 2x2x4 slice. The times are simulated.
32 devices in a mesh: seq: 8 (over z, x), dp: 4 (over y, core).
Axes of the slice: x: 2, y: 2, z: 4, core: 2. Of those that a mesh axis runs over, the one named last changes fastest.
Arguments:
- conv_input: bfloat16 [4, 2048, 2816], P('dp', 'seq'), may hold values from -6 to 6
- gate_input: bfloat16 [4, 2048, 2560], P('dp', 'seq'), may hold values from -6 to 6
- step_input: float32 [4, 40, 2048], P('dp', None, 'seq'), may hold values from -7.5 to 2048
- filter_taps: float32 [4, 2816], replicated, may hold values from -3 to 3
- filter_bias: float32 [2816], replicated, may hold values from -0.5 to 0.5
- step_bias: float32 [40], replicated, may hold values from -1 to 1
- decay_log: float32 [40], replicated, may hold values from -13 to 3
- skip_gain: float32 [40], replicated, may hold values from 0.5 to 1.5
- norm_weight: float32 [2560], replicated, may hold values from 0.5 to 1.5
- output_weight: bfloat16 [2560, 1280], P('dp'), may hold values from -0.125 to 0.125
- output_grad: bfloat16 [4, 2048, 1280], P('dp', 'seq'), may hold values from -6 to 6
Outputs:
- input_grad: bfloat16 [4, 2048, 2816], P('dp', 'seq')
- gate_grad: bfloat16 [4, 2048, 2560], P('dp', 'seq')
- step_grad: float32 [4, 40, 2048], P('dp', None, 'seq')
- weight_grad: float32 [2560, 1280], P('dp')
- filter_grads: float32 [5, 2816], replicated
- norm_grad: float32 [2560], replicated
- head_grads: float32 [3, 40], replicated
All inputs are finite; a program needn't handle non-finite values.
Results may differ from a plain program's by a relative error of at most 0.0029.
Values may be sent and summed in bfloat16 or wider, within the bound.
A program may use at most 192 MiB of HBM per device.

v0:
```python
import jax
import jax.numpy as jnp
from jax import lax
from jax.sharding import PartitionSpec as P

HEADS = 40
HEAD_DIM = 64
STATE = 128
SPAN = 256
INNER = 2560
PRECISE = lax.Precision.HIGH
MASKED = -1e30
EPSILON = 1e-05


def passed_along(value, axis, steps):
    count = lax.axis_size(axis)
    first, last = (max(0, -steps), min(count, count - steps))
    return lax.ppermute(value, axis, [(source, source + steps) for source in range(first, last)])


def spread(table, axis):
    count = lax.axis_size(axis)
    return lax.all_to_all(
        jnp.broadcast_to(table[None], (count,) + table.shape),
        axis,
        split_axis=0,
        concat_axis=0,
        tiled=True,
    )


def carried(states, decay_table, axis, reverse):
    count = lax.axis_size(axis)
    heads, features, width = states.shape
    pieces = states.reshape(heads, count, features // count, width).transpose(1, 0, 2, 3)
    pieces = lax.all_to_all(pieces, axis, split_axis=0, concat_axis=0, tiled=True)
    running = jnp.zeros(pieces.shape[1:], jnp.float32)
    found = [None] * count
    for at in reversed(range(count)) if reverse else range(count):
        found[at] = running
        running = decay_table[at][:, None, None] * running + pieces[at]
    back = lax.all_to_all(jnp.stack(found), axis, split_axis=0, concat_axis=0, tiled=True)
    return back.transpose(1, 0, 2, 3).reshape(heads, features, width)


def summed_everywhere(parts, axes):
    count = 1
    for axis in axes:
        count = count * lax.axis_size(axis)
    flat = jnp.concatenate([part.reshape(-1) for part in parts])
    chunk = -(-flat.shape[0] // (count * 128)) * 128
    padded = jnp.pad(flat, (0, chunk * count - flat.shape[0])).reshape(count, chunk)
    terms = lax.all_to_all(padded, axes, split_axis=0, concat_axis=0, tiled=True)
    total = lax.all_gather(jnp.sum(terms, axis=0), axes, axis=0, tiled=True)
    results, start = ([], 0)
    for part in parts:
        results.append(total[start : start + part.size].reshape(part.shape))
        start += part.size
    return results


def prepare(extended, step_rows, filter_taps, filter_bias, step_bias, decay_log):
    width = filter_taps.shape[0]
    length = extended.shape[0] - width + 1
    filtered = filter_bias + filter_taps[0] * extended[0:length]
    for offset in range(1, width):
        filtered = filtered + filter_taps[offset] * extended[offset : offset + length]
    activated = jax.nn.silu(filtered)
    step_sizes = jax.nn.softplus(step_rows + step_bias[:, None])
    decay_rates = step_sizes * (-jnp.exp(decay_log))[:, None]
    blocks = length // SPAN
    cumsums = jnp.cumsum(decay_rates.reshape(HEADS, blocks, SPAN), axis=2)
    values = activated[:, :INNER].reshape(blocks, SPAN, HEADS, HEAD_DIM)
    key_side = activated[:, INNER : INNER + STATE].reshape(blocks, SPAN, STATE)
    scaled = values * step_sizes.reshape(HEADS, blocks, SPAN).transpose(1, 2, 0)[..., None]
    to_end = jnp.exp(cumsums[:, :, -1:] - cumsums)
    block_states = jnp.einsum("hcs,cshp,csn->chpn", to_end, scaled, key_side, precision=PRECISE)
    decays = jnp.exp(cumsums[:, :, -1]).T
    return (activated, cumsums, scaled, block_states, decays)


def finish(
    activated, cumsums, scaled, block_states, decays, entering, skip_gain, gate_rows, norm_weight
):
    blocks = cumsums.shape[1]
    length = blocks * SPAN
    values = activated[:, :INNER].reshape(blocks, SPAN, HEADS, HEAD_DIM)
    key_side = activated[:, INNER : INNER + STATE].reshape(blocks, SPAN, STATE)
    query_side = activated[:, INNER + STATE :].reshape(blocks, SPAN, STATE)
    starting = []
    starting.append(entering)
    starting = jnp.stack(starting)
    scores = jnp.einsum("ctn,csn->cts", query_side, key_side, precision=PRECISE)
    differences = cumsums[:, :, :, None] - cumsums[:, :, None, :]
    causal = jnp.tril(jnp.ones((SPAN, SPAN), dtype=bool))
    weights = scores[None] * jnp.exp(jnp.where(causal, differences, MASKED))
    inside = jnp.einsum("hcts,cshp->cthp", weights, scaled, precision=PRECISE)
    from_state = (
        jnp.einsum("ctn,chpn->cthp", query_side, starting, precision=PRECISE)
        * jnp.exp(cumsums).transpose(1, 2, 0)[..., None]
    )
    result = inside + from_state + skip_gain[:, None] * values
    scanned = result.reshape(length, INNER)
    gated = scanned * jax.nn.silu(gate_rows)
    inverse_rms = lax.rsqrt(jnp.mean(gated * gated, axis=1, keepdims=True) + EPSILON)
    return gated * inverse_rms * norm_weight


def body(
    conv_input,
    gate_input,
    step_input,
    filter_taps,
    filter_bias,
    step_bias,
    decay_log,
    skip_gain,
    norm_weight,
    output_weight,
    output_grad,
):
    kernel_rows = filter_taps.shape[0] - 1
    raw_rows = conv_input[0]
    before = passed_along(raw_rows[-kernel_rows:], "seq", 1)
    extended = jnp.concatenate([before, raw_rows], axis=0).astype(jnp.float32)
    gate_rows = gate_input[0].astype(jnp.float32)
    step_rows = step_input[0]
    cotangent = output_grad[0]
    tokens = cotangent.shape[0]
    primals, pull_first = jax.vjp(
        prepare, extended, step_rows, filter_taps, filter_bias, step_bias, decay_log
    )
    activated, cumsums, scaled, block_states, decays = primals
    decay_table = spread(decays[0], "seq")
    entering = carried(block_states[0], decay_table, "seq", False)
    normed, pull_second = jax.vjp(
        finish,
        activated,
        cumsums,
        scaled,
        block_states,
        decays,
        entering,
        skip_gain,
        gate_rows,
        norm_weight,
    )
    normed_low = normed.astype(jnp.bfloat16)
    groups = lax.axis_size("dp")
    own_rows = output_weight.shape[0]
    everyone = lax.all_gather(cotangent, "dp", axis=0, tiled=True)
    partial_columns = lax.dot_general(
        everyone, output_weight, (((1,), (1,)), ((), ())), preferred_element_type=jnp.float32
    )
    regrouped = partial_columns.reshape(groups, tokens, own_rows)
    normed_grad = lax.all_to_all(regrouped, "dp", split_axis=0, concat_axis=2, tiled=True).reshape(
        tokens, groups * own_rows
    )
    own_columns = lax.all_to_all(normed_low, "dp", split_axis=1, concat_axis=0, tiled=True)
    weight_piece = lax.dot_general(
        own_columns, everyone, (((0,), (0,)), ((), ())), preferred_element_type=jnp.float32
    )
    spans = lax.axis_size("seq")
    weight_terms = lax.all_to_all(
        weight_piece.astype(jnp.bfloat16).reshape(spans, own_rows // spans, -1),
        "seq",
        split_axis=0,
        concat_axis=0,
        tiled=True,
    )
    weight_rows = jnp.sum(weight_terms.astype(jnp.float32), axis=0)
    weight_grad = lax.all_gather(weight_rows, "seq", axis=0, tiled=True)
    second = pull_second(normed_grad)
    (
        grad_activated,
        grad_cumsums,
        grad_scaled,
        grad_states,
        grad_decays,
        grad_entering,
        grad_skip,
        grad_gate,
        grad_norm,
    ) = second
    end_grad = carried(grad_entering, decay_table, "seq", True)
    decay_grad = jnp.sum(end_grad * entering, axis=(1, 2))
    first = pull_first(
        (
            grad_activated,
            grad_cumsums,
            grad_scaled,
            grad_states + end_grad[None],
            grad_decays + decay_grad[None],
        )
    )
    grad_extended, grad_steps, grad_taps, grad_bias, grad_step_bias, grad_decay_log = first
    returned = passed_along(grad_extended[:kernel_rows], "seq", -1)
    own_part = grad_extended[kernel_rows:]
    own_part = jnp.concatenate(
        [own_part[:-kernel_rows], own_part[-kernel_rows:] + returned], axis=0
    )
    filter_part = jnp.concatenate([grad_taps, grad_bias[None]], axis=0)
    head_part = jnp.stack([grad_step_bias, grad_decay_log, grad_skip])
    filter_grads, norm_grad, head_grads = summed_everywhere(
        (filter_part, grad_norm, head_part), ("seq", "dp")
    )
    input_grad = own_part.astype(jnp.bfloat16)[None]
    gate_grad = grad_gate.astype(jnp.bfloat16)[None]
    step_grad = grad_steps[None]
    return (input_grad, gate_grad, step_grad, weight_grad, filter_grads, norm_grad, head_grads)


def solution(mesh):
    return jax.shard_map(
        body,
        mesh=mesh,
        in_specs=(
            P("dp", "seq", None),
            P("dp", "seq", None),
            P("dp", None, "seq"),
            P(),
            P(),
            P(),
            P(),
            P(),
            P(),
            P("dp", None),
            P("dp", "seq", None),
        ),
        out_specs=(
            P("dp", "seq", None),
            P("dp", "seq", None),
            P("dp", None, "seq"),
            P("dp", None),
            P(),
            P(),
            P(),
        ),
        check_vma=False,
    )
```

profile of v0, /device:TPU:0, one launch (start us, length us, event | category | flops | bytes accessed | tf_op | source)
XLA Modules:
  0.0 410.9 jit_solution(12304909783855509701)
XLA Ops:
  8.1 4.9 %collective-permute-start = (bf16[3,2816]{1,0:T(4,128)(2,1)S(1)}, bf16[3,2816]{1,0:T(4,128)(2,1)S(1)}, u32[]{:S(2)}, u32[]{:S(2)}) collective-permute-start(bf16[3,2816]{1,0:T(4,128)(2,1)S(1)} %slice_bitcast_fusion), channel_id=1, source_target_pairs={{0,4},{4,8},{8,12},{12,16},{16,20},{20,24},{24,28},{1,5},{5,9},{9,... | collective-permute-start | bytes 50696 | tf_op jit(solution)/shard_map/ppermute | solution.py:19
  16.9 4.9 %all-to-all-start.1 = ((f32[8,1,40]{2,1,0:T(1,128)}), f32[8,1,40]{2,1,0:T(1,128)S(1)}, u32[]{:S(2)}, u32[]{:S(2)}) async-start(f32[8,1,40]{2,1,0:T(1,128)} %broadcast_in_dim.32), calls=%async_computation.1 | async-start | bytes 8192 | tf_op jit(solution)/shard_map/all_to_all | solution.py:24
  41.1 6.0 %all-to-all-start.2 = ((f32[8,40,8,128]{3,2,1,0:T(8,128)}), f32[8,40,8,128]{3,2,1,0:T(8,128)S(1)}, u32[]{:S(2)}, u32[]{:S(2)}) async-start(f32[8,40,8,128]{3,2,1,0:T(8,128)} %copy.225), calls=%async_computation.2 | async-start | bytes 2621440 | tf_op jit(solution)/shard_map/all_to_all | solution.py:37
  49.9 28.0 %all-to-all-done.2 = f32[8,40,8,128]{3,2,1,0:T(8,128)S(1)} async-done(((f32[8,40,8,128]{3,2,1,0:T(8,128)}), f32[8,40,8,128]{3,2,1,0:T(8,128)S(1)}, u32[]{:S(2)}, u32[]{:S(2)}) %all-to-all-start.2) | async-done | bytes 1310752 | tf_op jit(solution)/shard_map/all_to_all | solution.py:37
  87.1 5.5 %fusion.44 = f32[1024,640]{1,0:T(8,128)} fusion(bf16[640,1280]{1,0:T(8,128)(2,1)S(1)} %copy-done, bf16[1,1024,1280]{2,1,0:T(8,128)(2,1)} %all-gather.7.cloned.1.call-done), kind=kOutput, calls=%fused_computation.67 | convolution fusion | flops 1677721600 | bytes 6881280 | tf_op jit(solution)/shard_map/dot_general | solution.py:153
  92.6 25.8 %all-to-all-done.3 = f32[8,40,8,128]{3,2,1,0:T(8,128)S(1)} async-done(((f32[8,40,8,128]{3,2,1,0:T(8,128)}), f32[8,40,8,128]{3,2,1,0:T(8,128)S(1)}, u32[]{:S(2)}, u32[]{:S(2)}) %all-to-all-start.3) | async-done | bytes 1310752 | tf_op jit(solution)/shard_map/all_to_all | solution.py:43
  134.4 20.4 %all-to-all-done = f32[4,256,640]{2,1,0:T(8,128)S(1)} async-done(((f32[4,256,640]{2,1,0:T(8,128)}), f32[4,256,640]{2,1,0:T(8,128)S(1)}, u32[]{:S(2)}, u32[]{:S(2)}) %all-to-all-start) | async-done | bytes 2621472 | tf_op jit(solution)/shard_map/all_to_all | solution.py:157
  157.3 10.1 %multiply_reduce_fusion.9 = (f32[256]{0:T(256)S(1)}, f32[256]{0:T(256)S(1)}, f32[1,256,40,64]{1,3,2,0:T(8,128)S(1)}) fusion(f32[1,256,40,64]{1,3,2,0:T(8,128)} %bitcast.317, f32[1,256,40,64]{1,3,2,0:T(8,128)} %bitcast.329, f32[40,64]{1,0:T(8,128)S(1)} %mul.692, f32[1,256,40,64]{1,3,2,0:T(8,128)} %bitcast.323, f32[40]{0:T(128)S(1)} %copy-done.51, ...), kind=kOutput, calls=%fused_computation.74 | convolution fusion | flops 1024327168 | bytes 16191648 | tf_op jit(solution)/shard_map/jvp(hcts,cshp->cthp)/dot_general | solution.py:98
  169.4 4.3 %all-to-all-start.6 = ((bf16[256,4,640]{0,2,1:T(8,128)(2,1)}), bf16[256,4,640]{0,2,1:T(8,128)(2,1)}, u32[]{:S(2)}, u32[]{:S(2)}) async-start(bf16[256,4,640]{0,2,1:T(8,128)(2,1)} %multiply_convert_fusion), calls=%async_computation.6 | async-start | bytes 2621440 | tf_op jit(solution)/shard_map/all_to_all | solution.py:160
  173.7 4.2 %broadcast_multiply_fusion.5 = (f32[1,256,40,64]{1,3,2,0:T(8,128)}, f32[1,256,40,64]{1,3,2,0:T(8,128)S(1)}) fusion(f32[40]{0:T(128)S(1)} %copy-done.51, f32[256]{0:T(256)S(1)} %get-tuple-element.107, f32[1,256,40,64]{1,3,2,0:T(8,128)S(1)} %get-tuple-element.108, f32[1,256,40,64]{1,3,2,0:T(8,128)} %bitcast.318, f32[256]{0:T(256)S(1)} %get-tuple-element.106, ...), kind=kLoop, calls=%fused_computation.104 | loop fusion | flops 7864320 | bytes 13119648 | tf_op jit(solution)/shard_map/transpose(jvp())/mul | solution.py:103
  182.7 8.2 %all-to-all-done.6 = bf16[256,4,640]{0,2,1:T(8,128)(2,1)} async-done(((bf16[256,4,640]{0,2,1:T(8,128)(2,1)}), bf16[256,4,640]{0,2,1:T(8,128)(2,1)}, u32[]{:S(2)}, u32[]{:S(2)}) %all-to-all-start.6) | async-done | bytes 1310752 | tf_op jit(solution)/shard_map/all_to_all | solution.py:160
  191.0 4.3 %all-to-all-start.4 = ((f32[8,40,8,128]{3,2,1,0:T(8,128)}), f32[8,40,8,128]{3,2,1,0:T(8,128)}, u32[]{:S(2)}, u32[]{:S(2)}) async-start(f32[8,40,8,128]{3,2,1,0:T(8,128)} %copy.232), calls=%async_computation.4 | async-start | bytes 2621440 | tf_op jit(solution)/shard_map/all_to_all | solution.py:37
  200.9 5.3 %convolution_convert_fusion = bf16[640,1280]{1,0:T(8,128)(2,1)} fusion(bf16[1024,640]{1,0:T(8,128)(2,1)} %bitcast.342, bf16[1,1024,1280]{2,1,0:T(8,128)(2,1)} %all-gather.7.cloned.1.call-done), kind=kOutput, calls=%fused_computation.24 | convolution fusion | flops 1678540800 | bytes 5570560 | tf_op jit(solution)/shard_map/dot_general | solution.py:161
  206.2 20.4 %all-to-all-done.4 = f32[8,40,8,128]{3,2,1,0:T(8,128)} async-done(((f32[8,40,8,128]{3,2,1,0:T(8,128)}), f32[8,40,8,128]{3,2,1,0:T(8,128)}, u32[]{:S(2)}, u32[]{:S(2)}) %all-to-all-start.4) | async-done | bytes 1310752 | tf_op jit(solution)/shard_map/all_to_all | solution.py:37
  226.6 4.5 %all-to-all-start.7 = ((bf16[8,80,1280]{2,1,0:T(8,128)(2,1)}), bf16[8,80,1280]{2,1,0:T(8,128)(2,1)}, u32[]{:S(2)}, u32[]{:S(2)}) async-start(bf16[8,80,1280]{2,1,0:T(8,128)(2,1)} %bitcast.340), calls=%async_computation.7 | async-start | bytes 3276800 | tf_op jit(solution)/shard_map/all_to_all | solution.py:165
  231.1 4.3 %fusion.24 = bf16[1,256,2560]{1,2,0:T(8,128)(2,1)} fusion(f32[1,256,4,640]{1,3,2,0:T(8,128)} %copy.218, f32[1,256,40,64]{1,3,2,0:T(8,128)S(1)} %get-tuple-element.108, f32[256]{0:T(256)S(1)} %get-tuple-element.107, f32[256]{0:T(256)S(1)} %get-tuple-element.106, f32[2560]{0:T(1024)S(1)} %copy-done.25, bf16[1,256,2560]{1,2,0:T(8,128)(2,1)} %copy.229), kind=kLoop, calls=%fused_computation.40 | loop fusion | flops 12451840 | bytes 7876608 | tf_op jit(solution)/shard_map/convert_element_type | solution.py:209
  256.0 13.1 %all-to-all-done.7 = bf16[8,80,1280]{2,1,0:T(8,128)(2,1)} async-done(((bf16[8,80,1280]{2,1,0:T(8,128)(2,1)}), bf16[8,80,1280]{2,1,0:T(8,128)(2,1)}, u32[]{:S(2)}, u32[]{:S(2)}) %all-to-all-start.7) | async-done | bytes 1638432 | tf_op jit(solution)/shard_map/all_to_all | solution.py:165
  269.1 4.3 %all-to-all-start.5 = ((f32[8,40,8,128]{3,2,1,0:T(8,128)}), f32[8,40,8,128]{3,2,1,0:T(8,128)}, u32[]{:S(2)}, u32[]{:S(2)}) async-start(f32[8,40,8,128]{3,2,1,0:T(8,128)} %broadcast_dynamic-update-slice_fusion), calls=%async_computation.5 | async-start | bytes 2621440 | tf_op jit(solution)/shard_map/all_to_all | solution.py:43
  273.5 13.1 %fusion.6 = (f32[40,256]{1,0:T(8,128)}, f32[40,256]{1,0:T(8,128)S(1)}, f32[256,256]{1,0:T(8,128)S(1)}) fusion(f32[40,256]{1,0:T(8,128)} %get-tuple-element.88, f32[256,256]{1,0:T(8,128)S(1)} %copy-done.17, pred[256,256]{1,0:T(8,128)(4,1)} %copy-done.26, f32[256,40,64]{0,2,1:T(8,128)} %bitcast.325, f32[256,40]{0,1:T(8,128)S(1)} %fusion.124, ...), kind=kOutput, calls=%fused_computation.7 | convolution fusion | flops 1030795264 | bytes 5996544 | tf_op jit(solution)/shard_map/transpose(jvp(hcts,cshp->cthp))/dot_general | solution.py:98
  291.0 4.4 %multiply_reduce_fusion.6 = f32[4,640]{1,0:T(4,128)S(1)} fusion(f32[1,256,4,640]{3,1,2,0:T(8,128)} %copy.248, f32[1,256,4,640]{3,1,2,0:T(8,128)} %copy.247, f32[256]{0:T(256)S(1)} %copy-done.31, f32[4,256,640]{2,1,0:T(8,128)} %copy-done.6), kind=kLoop, calls=%fused_computation.70 | loop fusion | flops 5240320 | bytes 7875584 | tf_op jit(solution)/shard_map/transpose(jvp())/reduce_sum | solution.py:107
  311.5 7.5 %multiply_reduce_fusion.5 = (f32[40]{0:T(128)}, f32[256,40]{0,1:T(8,128)}, f32[1,256,40,64]{1,3,2,0:T(8,128)}) fusion(f32[1,256,40,64]{1,3,2,0:T(8,128)S(1)} %copy-done.9, f32[1,256,40,64]{1,3,2,0:T(8,128)S(1)} %bitcast.327, f32[256,40]{0,1:T(8,128)S(1)} %fusion.124, f32[256,40]{0,1:T(8,128)S(1)} %get-tuple-element.87, ...), kind=kOutput, calls=%fused_computation.69 | convolution fusion | flops 1019074560 | bytes 10977440 | tf_op jit(solution)/shard_map/transpose(jvp(hcts,cshp->cthp))/dot_general | solution.py:98
  325.9 5.4 %multiply_reduce_fusion.4 = (f32[2816]{0:T(1024)S(1)}, f32[2816]{0:T(1024)S(1)}, f32[2816]{0:T(1024)S(1)}, f32[2816]{0:T(1024)S(1)}, f32[2816]{0:T(1024)}, /*index=5*/f32[256,2816]{1,0:T(8,128)S(1)}) fusion(f32[259,2816]{1,0:T(8,128)S(1)} %copy-done.3, f32[256,2816]{1,0:T(8,128)} %get-tuple-element.90, f32[256,2560]{1,0:T(8,128)} %copy.235, ...), kind=kLoop, calls=%fused_computation.32 | loop fusion | flops 15845632 | bytes 22993920 | tf_op jit(solution)/shard_map/transpose(jvp())/reduce_sum | solution.py:68
  343.5 5.1 %all-to-all-start.8 = ((f32[32,1,640]{2,1,0:T(1,128)}), f32[32,1,640]{2,1,0:T(1,128)S(1)}, u32[]{:S(2)}, u32[]{:S(2)}) async-start(f32[32,1,640]{2,1,0:T(1,128)} %bitcast.102), calls=%async_computation.8 | async-start | bytes 163840 | tf_op jit(solution)/shard_map/all_to_all | solution.py:54
  357.9 40.0 %all-gather.1 = f32[32,1,640]{2,1,0:T(1,128)S(1)} all-gather(f32[1,1,640]{2,1,0:T(1,128)S(1)} %reshape.1035), channel_id=1, replica_groups=mesh['seq'=8,'dp'=4] {'seq','dp'}, dimensions={0}, use_global_device_ids=true | all-gather | bytes 84480 | tf_op jit(solution)/shard_map/all_gather | solution.py:55
  (236 shorter events, 141.9 us)
Async XLA Ops:
  7.2 79.9 %copy-start = (bf16[640,1280]{1,0:T(8,128)(2,1)S(1)}, bf16[640,1280]{1,0:T(8,128)(2,1)}, u32[]{:S(2)}) copy-start(bf16[640,1280]{1,0:T(8,128)(2,1)} %param.20) | copy-start | bytes 4915204
  8.1 16.8 %collective-permute-start = (bf16[3,2816]{1,0:T(4,128)(2,1)S(1)}, bf16[3,2816]{1,0:T(4,128)(2,1)S(1)}, u32[]{:S(2)}, u32[]{:S(2)}) collective-permute-start(bf16[3,2816]{1,0:T(4,128)(2,1)S(1)} %slice_bitcast_fusion), channel_id=1, source_target_pairs={{0,4},{4,8},{8,12},{12,16},{16,20},{20,24},{24,28},{1,5},{5,9},{9,... | collective-permute-start | bytes 50696 | tf_op jit(solution)/shard_map/ppermute | solution.py:19
  16.9 23.6 %all-to-all-start.1 = ((f32[8,1,40]{2,1,0:T(1,128)}), f32[8,1,40]{2,1,0:T(1,128)S(1)}, u32[]{:S(2)}, u32[]{:S(2)}) async-start(f32[8,1,40]{2,1,0:T(1,128)} %broadcast_in_dim.32), calls=%async_computation.1 | async-start | bytes 8192 | tf_op jit(solution)/shard_map/all_to_all | solution.py:24
  41.1 36.8 %all-to-all-start.2 = ((f32[8,40,8,128]{3,2,1,0:T(8,128)}), f32[8,40,8,128]{3,2,1,0:T(8,128)S(1)}, u32[]{:S(2)}, u32[]{:S(2)}) async-start(f32[8,40,8,128]{3,2,1,0:T(8,128)} %copy.225), calls=%async_computation.2 | async-start | bytes 2621440 | tf_op jit(solution)/shard_map/all_to_all | solution.py:37
  47.1 40.0 %all-gather.7.cloned.1.call-start = ((), (), s32[]{:S(2)}) async-start(), calls=%async_computation.10 | async-start | bytes 3276800 | tf_op jit(solution)/shard_map/all_gather | solution.py:152
  49.8 33.6 %copy-start.34 = (f32[40]{0:T(128)}, f32[40]{0:T(128)S(1)}, u32[]{:S(2)}) copy-start(f32[40]{0:T(128)S(1)} %get-tuple-element.100) | copy-start | bytes 484
  49.8 33.6 %copy-start.37 = (f32[40]{0:T(128)}, f32[40]{0:T(128)S(1)}, u32[]{:S(2)}) copy-start(f32[40]{0:T(128)S(1)} %get-tuple-element.102) | copy-start | bytes 484
  49.8 33.6 %copy-start.39 = (f32[40]{0:T(128)}, f32[40]{0:T(128)S(1)}, u32[]{:S(2)}) copy-start(f32[40]{0:T(128)S(1)} %get-tuple-element.101) | copy-start | bytes 484
  49.8 33.6 %copy-start.41 = (f32[40]{0:T(128)}, f32[40]{0:T(128)S(1)}, u32[]{:S(2)}) copy-start(f32[40]{0:T(128)S(1)} %get-tuple-element.103) | copy-start | bytes 484
  49.9 33.6 %copy-start.46 = (f32[40]{0:T(128)}, f32[40]{0:T(128)S(1)}, u32[]{:S(2)}) copy-start(f32[40]{0:T(128)S(1)} %get-tuple-element.99) | copy-start | bytes 484
  49.9 33.6 %copy-start.48 = (f32[40]{0:T(128)}, f32[40]{0:T(128)S(1)}, u32[]{:S(2)}) copy-start(f32[40]{0:T(128)S(1)} %get-tuple-element.104) | copy-start | bytes 484
  83.4 35.0 %all-to-all-start.3 = ((f32[8,40,8,128]{3,2,1,0:T(8,128)}), f32[8,40,8,128]{3,2,1,0:T(8,128)S(1)}, u32[]{:S(2)}, u32[]{:S(2)}) async-start(f32[8,40,8,128]{3,2,1,0:T(8,128)} %fusion.100), calls=%async_computation.3 | async-start | bytes 2621440 | tf_op jit(solution)/shard_map/all_to_all | solution.py:43
  119.5 35.4 %all-to-all-start = ((f32[4,256,640]{2,1,0:T(8,128)}), f32[4,256,640]{2,1,0:T(8,128)S(1)}, u32[]{:S(2)}, u32[]{:S(2)}) async-start(f32[4,256,640]{2,1,0:T(8,128)} %bitcast.338), calls=%async_computation | async-start | bytes 5242880 | tf_op jit(solution)/shard_map/all_to_all | solution.py:157
  123.8 54.2 %copy-start.14 = (f32[256,40]{0,1:T(8,128)}, f32[256,40]{0,1:T(8,128)S(1)}, u32[]{:S(2)}) copy-start(f32[256,40]{0,1:T(8,128)S(1)} %copy.227) | copy-start | bytes 122884
  129.4 27.9 %copy-start.26 = (pred[256,256]{1,0:T(8,128)(4,1)}, pred[256,256]{1,0:T(8,128)(4,1)S(1)}, u32[]{:S(2)}) copy-start(pred[256,256]{1,0:T(8,128)(4,1)S(1)} %iota_compare_fusion) | copy-start | bytes 196612
  130.7 26.6 %copy-start.16 = (f32[256,256]{1,0:T(8,128)}, f32[256,256]{1,0:T(8,128)S(1)}, u32[]{:S(2)}) copy-start(f32[256,256]{1,0:T(8,128)S(1)} %fusion.115) | copy-start | bytes 786436
  167.4 70.4 %copy-start.30 = (f32[256]{0:T(256)}, f32[256]{0:T(256)S(1)}, u32[]{:S(2)}) copy-start(f32[256]{0:T(256)S(1)} %get-tuple-element.106) | copy-start | bytes 3076
  169.4 21.6 %all-to-all-start.6 = ((bf16[256,4,640]{0,2,1:T(8,128)(2,1)}), bf16[256,4,640]{0,2,1:T(8,128)(2,1)}, u32[]{:S(2)}, u32[]{:S(2)}) async-start(bf16[256,4,640]{0,2,1:T(8,128)(2,1)} %multiply_convert_fusion), calls=%async_computation.6 | async-start | bytes 2621440 | tf_op jit(solution)/shard_map/all_to_all | solution.py:160
  191.0 35.6 %all-to-all-start.4 = ((f32[8,40,8,128]{3,2,1,0:T(8,128)}), f32[8,40,8,128]{3,2,1,0:T(8,128)}, u32[]{:S(2)}, u32[]{:S(2)}) async-start(f32[8,40,8,128]{3,2,1,0:T(8,128)} %copy.232), calls=%async_computation.4 | async-start | bytes 2621440 | tf_op jit(solution)/shard_map/all_to_all | solution.py:37
  226.6 42.5 %all-to-all-start.7 = ((bf16[8,80,1280]{2,1,0:T(8,128)(2,1)}), bf16[8,80,1280]{2,1,0:T(8,128)(2,1)}, u32[]{:S(2)}, u32[]{:S(2)}) async-start(bf16[8,80,1280]{2,1,0:T(8,128)(2,1)} %bitcast.340), calls=%async_computation.7 | async-start | bytes 3276800 | tf_op jit(solution)/shard_map/all_to_all | solution.py:165
  269.1 35.6 %all-to-all-start.5 = ((f32[8,40,8,128]{3,2,1,0:T(8,128)}), f32[8,40,8,128]{3,2,1,0:T(8,128)}, u32[]{:S(2)}, u32[]{:S(2)}) async-start(f32[8,40,8,128]{3,2,1,0:T(8,128)} %broadcast_dynamic-update-slice_fusion), calls=%async_computation.5 | async-start | bytes 2621440 | tf_op jit(solution)/shard_map/all_to_all | solution.py:43
  273.4 126.6 %all-gather.5.cloned.1.call-start = ((), (), s32[]{:S(2)}) async-start(), calls=%async_computation.9 | async-start | bytes 3686400 | tf_op jit(solution)/shard_map/all_gather | solution.py:173
  343.5 14.4 %all-to-all-start.8 = ((f32[32,1,640]{2,1,0:T(1,128)}), f32[32,1,640]{2,1,0:T(1,128)S(1)}, u32[]{:S(2)}, u32[]{:S(2)}) async-start(f32[32,1,640]{2,1,0:T(1,128)} %bitcast.102), calls=%async_computation.8 | async-start | bytes 163840 | tf_op jit(solution)/shard_map/all_to_all | solution.py:54
  350.3 6.3 %collective-permute-start.1 = (f32[3,2816]{1,0:T(4,128)S(1)}, f32[3,2816]{1,0:T(4,128)S(1)}, u32[]{:S(2)}, u32[]{:S(2)}) collective-permute-start(f32[3,2816]{1,0:T(4,128)S(1)} %pad_add_fusion.1), channel_id=1, source_target_pairs={{4,0},{8,4},{12,8},{16,12},{20,16},{24,20},{28,24},{5,1},{9,5},{13... | collective-permute-start | bytes 101384 | tf_op jit(solution)/shard_map/ppermute | solution.py:19
  (41 other events, 201.0 us)
Sparse Core Ops, SparseCore 0:
  49.4 26.9 all-gather.6
  304.8 62.9 all-gather.4
where the time goes:
time: 418 us; the launch traced here: 411 us
  waiting for transfers between devices  120 us (29%)
  other arithmetic  69.1 us (17%)
  matrix products  64.5 us (15%)
  local copies, waits for them, and re-layouts  54.6 us (13%)
  starting transfers between devices  47.2 us (11%)
  blocking collectives  40 us (10%)
  between operations  15.1 us (4%)
    all_to_all x2, waiting for transfers between devices, carried(): lax.all_to_all(pieces, axis, split_axis=0, concat_axis=0, tiled=True)  48.4 us
    all_gather x1, blocking collectives, summed_everywhere(): total = lax.all_gather(jnp.sum(terms, axis=0), axes, axis=0, tiled=True)  40 us
    dot_general x3, matrix products, finish(): inside = jnp.einsum('hcts,cshp->cthp', weights, scaled, precision=PRECISE)  30.7 us
    all_to_all x2, waiting for transfers between devices, carried(): lax.all_to_all(jnp.stack(found), axis, split_axis=0, concat_axis=0, tiled...  25.8 us
    all_to_all x1, waiting for transfers between devices, body(): lax.all_to_all(regrouped, 'dp', split_axis=0, concat_axis=2, tiled=True)  20.4 us
    unnamed x113, local copies, waits for them, and re-layouts  17.5 us
    all_to_all x1, waiting for transfers between devices, body(): lax.all_to_all(weight_piece.astype(jnp.bfloat16).reshape(spans, own_rows...  13.1 us
    unnamed x10, other arithmetic  12.2 us
  transfers between devices with their start and end apart: 13, of which 7 were waited for; matrix products, arithmetic and copies ran while one was open for 40% of the time, Pallas kernels for 0%

commit v1 on v0

--- a/solution.py
+++ b/solution.py
@@ -52,7 +52,9 @@
     chunk = -(-flat.shape[0] // (count * 128)) * 128
     padded = jnp.pad(flat, (0, chunk * count - flat.shape[0])).reshape(count, chunk)
     terms = lax.all_to_all(padded, axes, split_axis=0, concat_axis=0, tiled=True)
-    total = lax.all_gather(jnp.sum(terms, axis=0), axes, axis=0, tiled=True)
+    x = jnp.sum(terms, axis=0)
+    outgoing = jnp.stack([x] * lax.axis_size(axes))
+    total = jnp.concatenate(lax.all_to_all(outgoing, axes, 0, 0), axis=0)
     results, start = ([], 0)
     for part in parts:
         results.append(total[start : start + part.size].reshape(part.shape))

time: 418 us -> 391 us (0.935)
  blocking collectives: 40 us -> 0 us
  waiting for transfers between devices: 120 us -> 130 us
    all_gather x1 -> x0, blocking collectives: 40 us -> none  [summed_everywhere(): total = lax.all_gather(jnp.sum(terms, axis=0), axes, axis=0, tiled=True)]
    all_to_all x1, waiting for transfers between devices: 0.01 us -> 7.4 us  [summed_everywhere(): lax.all_to_all(padded, axes, split_axis=0, concat_axis=0, tiled=True)]
    all_to_all x0 -> x1, waiting for transfers between devices: none -> 5.81 us  [summed_everywhere(): total = jnp.concatenate(lax.all_to_all(outgoing, axes, 0, 0), axis=0)]
    unnamed x113 -> x148, local copies, waits for them, and re-layouts: 17.5 us -> 17.5 us
  transfers between devices with their start and end apart: 13 -> 14, of which waited for: 7 -> 8; matrix products, arithmetic and copies ran while one was open for 40% -> 43% of each run, Pallas kernels for 0% -> 0%
where the time goes in v1:
time: 391 us; the launch traced here: 384 us
  waiting for transfers between devices  130 us (33%)
  other arithmetic  68.9 us (18%)
  matrix products  64.5 us (16%)
  local copies, waits for them, and re-layouts  55 us (14%)
  starting transfers between devices  50.6 us (13%)
  between operations  15.4 us (4%)
    all_to_all x2, waiting for transfers between devices, carried(): lax.all_to_all(pieces, axis, split_axis=0, concat_axis=0, tiled=True)  48.4 us
    dot_general x3, matrix products, finish(): inside = jnp.einsum('hcts,cshp->cthp', weights, scaled, precision=PRECISE)  30.7 us
    all_to_all x2, waiting for transfers between devices, carried(): lax.all_to_all(jnp.stack(found), axis, split_axis=0, concat_axis=0, tiled...  25.9 us
    all_to_all x1, waiting for transfers between devices, body(): lax.all_to_all(regrouped, 'dp', split_axis=0, concat_axis=2, tiled=True)  20.4 us
    unnamed x148, local copies, waits for them, and re-layouts  17.5 us
    all_to_all x1, waiting for transfers between devices, body(): lax.all_to_all(weight_piece.astype(jnp.bfloat16).reshape(spans, own_rows...  13 us
    unnamed x10, other arithmetic  12.3 us
    all_to_all x2, starting transfers between devices, carried(): lax.all_to_all(pieces, axis, split_axis=0, concat_axis=0, tiled=True)  10.3 us
  transfers between devices with their start and end apart: 14, of which 8 were waited for; matrix products, arithmetic and copies ran while one was open for 43% of the time, Pallas kernels for 0%

profile of v1, /device:TPU:0, one launch (start us, length us, event | category | flops | bytes accessed | tf_op | source)
XLA Modules:
  0.0 384.3 jit_solution(12091787677952692931)
XLA Ops:
  8.1 4.9 %collective-permute-start = (bf16[3,2816]{1,0:T(4,128)(2,1)S(1)}, bf16[3,2816]{1,0:T(4,128)(2,1)S(1)}, u32[]{:S(2)}, u32[]{:S(2)}) collective-permute-start(bf16[3,2816]{1,0:T(4,128)(2,1)S(1)} %slice_bitcast_fusion), channel_id=1, source_target_pairs={{0,4},{4,8},{8,12},{12,16},{16,20},{20,24},{24,28},{1,5},{5,9},{9,... | collective-permute-start | bytes 50696 | tf_op jit(solution)/shard_map/ppermute | solution.py:19
  16.9 4.9 %all-to-all-start.1 = ((f32[8,1,40]{2,1,0:T(1,128)}), f32[8,1,40]{2,1,0:T(1,128)S(1)}, u32[]{:S(2)}, u32[]{:S(2)}) async-start(f32[8,1,40]{2,1,0:T(1,128)} %broadcast_in_dim.32), calls=%async_computation.1 | async-start | bytes 8192 | tf_op jit(solution)/shard_map/all_to_all | solution.py:24
  41.2 6.0 %all-to-all-start.2 = ((f32[8,40,8,128]{3,2,1,0:T(8,128)}), f32[8,40,8,128]{3,2,1,0:T(8,128)S(1)}, u32[]{:S(2)}, u32[]{:S(2)}) async-start(f32[8,40,8,128]{3,2,1,0:T(8,128)} %copy.225), calls=%async_computation.2 | async-start | bytes 2621440 | tf_op jit(solution)/shard_map/all_to_all | solution.py:37
  50.0 28.0 %all-to-all-done.2 = f32[8,40,8,128]{3,2,1,0:T(8,128)S(1)} async-done(((f32[8,40,8,128]{3,2,1,0:T(8,128)}), f32[8,40,8,128]{3,2,1,0:T(8,128)S(1)}, u32[]{:S(2)}, u32[]{:S(2)}) %all-to-all-start.2) | async-done | bytes 1310752 | tf_op jit(solution)/shard_map/all_to_all | solution.py:37
  87.2 5.5 %fusion.44 = f32[1024,640]{1,0:T(8,128)} fusion(bf16[640,1280]{1,0:T(8,128)(2,1)S(1)} %copy-done, bf16[1,1024,1280]{2,1,0:T(8,128)(2,1)} %all-gather.6.cloned.1.call-done), kind=kOutput, calls=%fused_computation.67 | convolution fusion | flops 1677721600 | bytes 6881280 | tf_op jit(solution)/shard_map/dot_general | solution.py:155
  92.7 25.9 %all-to-all-done.3 = f32[8,40,8,128]{3,2,1,0:T(8,128)S(1)} async-done(((f32[8,40,8,128]{3,2,1,0:T(8,128)}), f32[8,40,8,128]{3,2,1,0:T(8,128)S(1)}, u32[]{:S(2)}, u32[]{:S(2)}) %all-to-all-start.3) | async-done | bytes 1310752 | tf_op jit(solution)/shard_map/all_to_all | solution.py:43
  134.6 20.4 %all-to-all-done = f32[4,256,640]{2,1,0:T(8,128)S(1)} async-done(((f32[4,256,640]{2,1,0:T(8,128)}), f32[4,256,640]{2,1,0:T(8,128)S(1)}, u32[]{:S(2)}, u32[]{:S(2)}) %all-to-all-start) | async-done | bytes 2621472 | tf_op jit(solution)/shard_map/all_to_all | solution.py:159
  157.5 10.2 %multiply_reduce_fusion.9 = (f32[256]{0:T(256)S(1)}, f32[256]{0:T(256)S(1)}, f32[1,256,40,64]{1,3,2,0:T(8,128)S(1)}) fusion(f32[1,256,40,64]{1,3,2,0:T(8,128)} %bitcast.316, f32[1,256,40,64]{1,3,2,0:T(8,128)} %bitcast.328, f32[40,64]{1,0:T(8,128)S(1)} %mul.692, f32[1,256,40,64]{1,3,2,0:T(8,128)} %bitcast.322, f32[40]{0:T(128)S(1)} %copy-done.68, ...), kind=kOutput, calls=%fused_computation.74 | convolution fusion | flops 1024327168 | bytes 16191648 | tf_op jit(solution)/shard_map/jvp(hcts,cshp->cthp)/dot_general | solution.py:100
  169.6 4.3 %all-to-all-start.6 = ((bf16[256,4,640]{0,2,1:T(8,128)(2,1)}), bf16[256,4,640]{0,2,1:T(8,128)(2,1)}, u32[]{:S(2)}, u32[]{:S(2)}) async-start(bf16[256,4,640]{0,2,1:T(8,128)(2,1)} %multiply_convert_fusion), calls=%async_computation.6 | async-start | bytes 2621440 | tf_op jit(solution)/shard_map/all_to_all | solution.py:162
  182.9 8.3 %all-to-all-done.6 = bf16[256,4,640]{0,2,1:T(8,128)(2,1)} async-done(((bf16[256,4,640]{0,2,1:T(8,128)(2,1)}), bf16[256,4,640]{0,2,1:T(8,128)(2,1)}, u32[]{:S(2)}, u32[]{:S(2)}) %all-to-all-start.6) | async-done | bytes 1310752 | tf_op jit(solution)/shard_map/all_to_all | solution.py:162
  191.2 4.3 %all-to-all-start.4 = ((f32[8,40,8,128]{3,2,1,0:T(8,128)}), f32[8,40,8,128]{3,2,1,0:T(8,128)}, u32[]{:S(2)}, u32[]{:S(2)}) async-start(f32[8,40,8,128]{3,2,1,0:T(8,128)} %copy.232), calls=%async_computation.4 | async-start | bytes 2621440 | tf_op jit(solution)/shard_map/all_to_all | solution.py:37
  201.2 5.2 %convolution_convert_fusion = bf16[640,1280]{1,0:T(8,128)(2,1)} fusion(bf16[1024,640]{1,0:T(8,128)(2,1)} %bitcast.341, bf16[1,1024,1280]{2,1,0:T(8,128)(2,1)} %all-gather.6.cloned.1.call-done), kind=kOutput, calls=%fused_computation.24 | convolution fusion | flops 1678540800 | bytes 5570560 | tf_op jit(solution)/shard_map/dot_general | solution.py:163
  206.4 20.5 %all-to-all-done.4 = f32[8,40,8,128]{3,2,1,0:T(8,128)} async-done(((f32[8,40,8,128]{3,2,1,0:T(8,128)}), f32[8,40,8,128]{3,2,1,0:T(8,128)}, u32[]{:S(2)}, u32[]{:S(2)}) %all-to-all-start.4) | async-done | bytes 1310752 | tf_op jit(solution)/shard_map/all_to_all | solution.py:37
  226.9 4.5 %all-to-all-start.7 = ((bf16[8,80,1280]{2,1,0:T(8,128)(2,1)}), bf16[8,80,1280]{2,1,0:T(8,128)(2,1)}, u32[]{:S(2)}, u32[]{:S(2)}) async-start(bf16[8,80,1280]{2,1,0:T(8,128)(2,1)} %bitcast.339), calls=%async_computation.7 | async-start | bytes 3276800 | tf_op jit(solution)/shard_map/all_to_all | solution.py:167
  231.4 4.4 %fusion.24 = bf16[1,256,2560]{1,2,0:T(8,128)(2,1)} fusion(f32[1,256,4,640]{1,3,2,0:T(8,128)} %copy.218, f32[1,256,40,64]{1,3,2,0:T(8,128)S(1)} %get-tuple-element.108, f32[256]{0:T(256)S(1)} %get-tuple-element.107, f32[256]{0:T(256)S(1)} %get-tuple-element.106, f32[2560]{0:T(1024)S(1)} %copy-done.36, bf16[1,256,2560]{1,2,0:T(8,128)(2,1)} %copy.229), kind=kLoop, calls=%fused_computation.40 | loop fusion | flops 12451840 | bytes 7876608 | tf_op jit(solution)/shard_map/convert_element_type | solution.py:211
  256.4 13.0 %all-to-all-done.7 = bf16[8,80,1280]{2,1,0:T(8,128)(2,1)} async-done(((bf16[8,80,1280]{2,1,0:T(8,128)(2,1)}), bf16[8,80,1280]{2,1,0:T(8,128)(2,1)}, u32[]{:S(2)}, u32[]{:S(2)}) %all-to-all-start.7) | async-done | bytes 1638432 | tf_op jit(solution)/shard_map/all_to_all | solution.py:167
  269.4 4.3 %all-to-all-start.5 = ((f32[8,40,8,128]{3,2,1,0:T(8,128)}), f32[8,40,8,128]{3,2,1,0:T(8,128)}, u32[]{:S(2)}, u32[]{:S(2)}) async-start(f32[8,40,8,128]{3,2,1,0:T(8,128)} %broadcast_dynamic-update-slice_fusion), calls=%async_computation.5 | async-start | bytes 2621440 | tf_op jit(solution)/shard_map/all_to_all | solution.py:43
  273.7 13.1 %fusion.6 = (f32[40,256]{1,0:T(8,128)}, f32[40,256]{1,0:T(8,128)S(1)}, f32[256,256]{1,0:T(8,128)S(1)}) fusion(f32[40,256]{1,0:T(8,128)} %get-tuple-element.88, f32[256,256]{1,0:T(8,128)S(1)} %copy-done.23, pred[256,256]{1,0:T(8,128)(4,1)} %copy-done.37, f32[256,40,64]{0,2,1:T(8,128)} %bitcast.324, f32[256,40]{0,1:T(8,128)S(1)} %fusion.124, ...), kind=kOutput, calls=%fused_computation.7 | convolution fusion | flops 1030795264 | bytes 5996544 | tf_op jit(solution)/shard_map/transpose(jvp(hcts,cshp->cthp))/dot_general | solution.py:100
  291.3 4.4 %multiply_reduce_fusion.6 = f32[4,640]{1,0:T(4,128)S(1)} fusion(f32[1,256,4,640]{3,1,2,0:T(8,128)} %copy.248, f32[1,256,4,640]{3,1,2,0:T(8,128)} %copy.247, f32[256]{0:T(256)S(1)} %copy-done.43, f32[4,256,640]{2,1,0:T(8,128)} %copy-done.9), kind=kLoop, calls=%fused_computation.70 | loop fusion | flops 5240320 | bytes 7875584 | tf_op jit(solution)/shard_map/transpose(jvp())/reduce_sum | solution.py:109
  311.7 7.5 %multiply_reduce_fusion.5 = (f32[40]{0:T(128)}, f32[256,40]{0,1:T(8,128)}, f32[1,256,40,64]{1,3,2,0:T(8,128)}) fusion(f32[1,256,40,64]{1,3,2,0:T(8,128)S(1)} %copy-done.12, f32[1,256,40,64]{1,3,2,0:T(8,128)S(1)} %bitcast.326, f32[256,40]{0,1:T(8,128)S(1)} %fusion.124, f32[256,40]{0,1:T(8,128)S(1)} %get-tuple-element.87, ...), kind=kOutput, calls=%fused_computation.69 | convolution fusion | flops 1019074560 | bytes 10977440 | tf_op jit(solution)/shard_map/transpose(jvp(hcts,cshp->cthp))/dot_general | solution.py:100
  326.2 6.0 %multiply_reduce_fusion.4 = (f32[2816]{0:T(1024)S(1)}, f32[2816]{0:T(1024)S(1)}, f32[2816]{0:T(1024)S(1)}, f32[2816]{0:T(1024)S(1)}, f32[2816]{0:T(1024)S(1)}, /*index=5*/f32[256,2816]{1,0:T(8,128)}) fusion(f32[259,2816]{1,0:T(8,128)S(1)} %copy-done.3, f32[256,2816]{1,0:T(8,128)} %get-tuple-element.90, f32[256,2560]{1,0:T(8,128)} %copy.235, ...), kind=kLoop, calls=%fused_computation.32 | loop fusion | flops 15845632 | bytes 22993920 | tf_op jit(solution)/shard_map/transpose(jvp())/reduce_sum | solution.py:70
  345.1 5.7 %all-to-all-start.8 = ((f32[32,1,640]{2,1,0:T(1,128)}), f32[32,1,640]{2,1,0:T(1,128)S(1)}, u32[]{:S(2)}, u32[]{:S(2)}) async-start(f32[32,1,640]{2,1,0:T(1,128)} %bitcast.102), calls=%async_computation.8 | async-start | bytes 163840 | tf_op jit(solution)/shard_map/all_to_all | solution.py:54
  351.8 7.4 %all-to-all-done.8 = f32[32,1,640]{2,1,0:T(1,128)S(1)} async-done(((f32[32,1,640]{2,1,0:T(1,128)}), f32[32,1,640]{2,1,0:T(1,128)S(1)}, u32[]{:S(2)}, u32[]{:S(2)}) %all-to-all-start.8) | async-done | bytes 81952 | tf_op jit(solution)/shard_map/all_to_all | solution.py:54
  365.1 5.8 %all-to-all-done.9 = f32[32,1,640]{2,1,0:T(1,128)S(1)} async-done(((f32[32,1,640]{2,1,0:T(1,128)}), f32[32,1,640]{2,1,0:T(1,128)S(1)}, u32[]{:S(2)}, u32[]{:S(2)}) %all-to-all-start.9) | async-done | bytes 81952 | tf_op jit(solution)/shard_map/all_to_all | solution.py:57
  (274 shorter events, 144.7 us)
Async XLA Ops:
  7.2 80.0 %copy-start = (bf16[640,1280]{1,0:T(8,128)(2,1)S(1)}, bf16[640,1280]{1,0:T(8,128)(2,1)}, u32[]{:S(2)}) copy-start(bf16[640,1280]{1,0:T(8,128)(2,1)} %param.20) | copy-start | bytes 4915204
  8.1 16.9 %collective-permute-start = (bf16[3,2816]{1,0:T(4,128)(2,1)S(1)}, bf16[3,2816]{1,0:T(4,128)(2,1)S(1)}, u32[]{:S(2)}, u32[]{:S(2)}) collective-permute-start(bf16[3,2816]{1,0:T(4,128)(2,1)S(1)} %slice_bitcast_fusion), channel_id=1, source_target_pairs={{0,4},{4,8},{8,12},{12,16},{16,20},{20,24},{24,28},{1,5},{5,9},{9,... | collective-permute-start | bytes 50696 | tf_op jit(solution)/shard_map/ppermute | solution.py:19
  16.9 23.7 %all-to-all-start.1 = ((f32[8,1,40]{2,1,0:T(1,128)}), f32[8,1,40]{2,1,0:T(1,128)S(1)}, u32[]{:S(2)}, u32[]{:S(2)}) async-start(f32[8,1,40]{2,1,0:T(1,128)} %broadcast_in_dim.32), calls=%async_computation.1 | async-start | bytes 8192 | tf_op jit(solution)/shard_map/all_to_all | solution.py:24
  41.2 36.8 %all-to-all-start.2 = ((f32[8,40,8,128]{3,2,1,0:T(8,128)}), f32[8,40,8,128]{3,2,1,0:T(8,128)S(1)}, u32[]{:S(2)}, u32[]{:S(2)}) async-start(f32[8,40,8,128]{3,2,1,0:T(8,128)} %copy.225), calls=%async_computation.2 | async-start | bytes 2621440 | tf_op jit(solution)/shard_map/all_to_all | solution.py:37
  47.2 40.0 %all-gather.6.cloned.1.call-start = ((), (), s32[]{:S(2)}) async-start(), calls=%async_computation.11 | async-start | bytes 3276800 | tf_op jit(solution)/shard_map/all_gather | solution.py:154
  50.0 33.6 %copy-start.46 = (f32[40]{0:T(128)}, f32[40]{0:T(128)S(1)}, u32[]{:S(2)}) copy-start(f32[40]{0:T(128)S(1)} %get-tuple-element.100) | copy-start | bytes 484
  50.0 33.6 %copy-start.49 = (f32[40]{0:T(128)}, f32[40]{0:T(128)S(1)}, u32[]{:S(2)}) copy-start(f32[40]{0:T(128)S(1)} %get-tuple-element.102) | copy-start | bytes 484
  50.0 33.6 %copy-start.51 = (f32[40]{0:T(128)}, f32[40]{0:T(128)S(1)}, u32[]{:S(2)}) copy-start(f32[40]{0:T(128)S(1)} %get-tuple-element.101) | copy-start | bytes 484
  50.0 33.6 %copy-start.53 = (f32[40]{0:T(128)}, f32[40]{0:T(128)S(1)}, u32[]{:S(2)}) copy-start(f32[40]{0:T(128)S(1)} %get-tuple-element.103) | copy-start | bytes 484
  50.0 33.6 %copy-start.60 = (f32[40]{0:T(128)}, f32[40]{0:T(128)S(1)}, u32[]{:S(2)}) copy-start(f32[40]{0:T(128)S(1)} %get-tuple-element.99) | copy-start | bytes 484
  50.0 33.6 %copy-start.62 = (f32[40]{0:T(128)}, f32[40]{0:T(128)S(1)}, u32[]{:S(2)}) copy-start(f32[40]{0:T(128)S(1)} %get-tuple-element.104) | copy-start | bytes 484
  83.6 35.0 %all-to-all-start.3 = ((f32[8,40,8,128]{3,2,1,0:T(8,128)}), f32[8,40,8,128]{3,2,1,0:T(8,128)S(1)}, u32[]{:S(2)}, u32[]{:S(2)}) async-start(f32[8,40,8,128]{3,2,1,0:T(8,128)} %fusion.100), calls=%async_computation.3 | async-start | bytes 2621440 | tf_op jit(solution)/shard_map/all_to_all | solution.py:43
  119.6 35.4 %all-to-all-start = ((f32[4,256,640]{2,1,0:T(8,128)}), f32[4,256,640]{2,1,0:T(8,128)S(1)}, u32[]{:S(2)}, u32[]{:S(2)}) async-start(f32[4,256,640]{2,1,0:T(8,128)} %bitcast.337), calls=%async_computation | async-start | bytes 5242880 | tf_op jit(solution)/shard_map/all_to_all | solution.py:159
  123.9 54.3 %copy-start.20 = (f32[256,40]{0,1:T(8,128)}, f32[256,40]{0,1:T(8,128)S(1)}, u32[]{:S(2)}) copy-start(f32[256,40]{0,1:T(8,128)S(1)} %copy.227) | copy-start | bytes 122884
  129.5 27.9 %copy-start.37 = (pred[256,256]{1,0:T(8,128)(4,1)}, pred[256,256]{1,0:T(8,128)(4,1)S(1)}, u32[]{:S(2)}) copy-start(pred[256,256]{1,0:T(8,128)(4,1)S(1)} %iota_compare_fusion) | copy-start | bytes 196612
  167.7 70.5 %copy-start.42 = (f32[256]{0:T(256)}, f32[256]{0:T(256)S(1)}, u32[]{:S(2)}) copy-start(f32[256]{0:T(256)S(1)} %get-tuple-element.106) | copy-start | bytes 3076
  169.6 21.6 %all-to-all-start.6 = ((bf16[256,4,640]{0,2,1:T(8,128)(2,1)}), bf16[256,4,640]{0,2,1:T(8,128)(2,1)}, u32[]{:S(2)}, u32[]{:S(2)}) async-start(bf16[256,4,640]{0,2,1:T(8,128)(2,1)} %multiply_convert_fusion), calls=%async_computation.6 | async-start | bytes 2621440 | tf_op jit(solution)/shard_map/all_to_all | solution.py:162
  191.2 35.6 %all-to-all-start.4 = ((f32[8,40,8,128]{3,2,1,0:T(8,128)}), f32[8,40,8,128]{3,2,1,0:T(8,128)}, u32[]{:S(2)}, u32[]{:S(2)}) async-start(f32[8,40,8,128]{3,2,1,0:T(8,128)} %copy.232), calls=%async_computation.4 | async-start | bytes 2621440 | tf_op jit(solution)/shard_map/all_to_all | solution.py:37
  226.9 42.5 %all-to-all-start.7 = ((bf16[8,80,1280]{2,1,0:T(8,128)(2,1)}), bf16[8,80,1280]{2,1,0:T(8,128)(2,1)}, u32[]{:S(2)}, u32[]{:S(2)}) async-start(bf16[8,80,1280]{2,1,0:T(8,128)(2,1)} %bitcast.339), calls=%async_computation.7 | async-start | bytes 3276800 | tf_op jit(solution)/shard_map/all_to_all | solution.py:167
  269.4 35.6 %all-to-all-start.5 = ((f32[8,40,8,128]{3,2,1,0:T(8,128)}), f32[8,40,8,128]{3,2,1,0:T(8,128)}, u32[]{:S(2)}, u32[]{:S(2)}) async-start(f32[8,40,8,128]{3,2,1,0:T(8,128)} %broadcast_dynamic-update-slice_fusion), calls=%async_computation.5 | async-start | bytes 2621440 | tf_op jit(solution)/shard_map/all_to_all | solution.py:43
  273.7 99.7 %all-gather.4.cloned.1.call-start = ((), (), s32[]{:S(2)}) async-start(), calls=%async_computation.10 | async-start | bytes 3686400 | tf_op jit(solution)/shard_map/all_gather | solution.py:175
  338.9 12.0 %collective-permute-start.1 = (f32[3,2816]{1,0:T(4,128)S(1)}, f32[3,2816]{1,0:T(4,128)S(1)}, u32[]{:S(2)}, u32[]{:S(2)}) collective-permute-start(f32[3,2816]{1,0:T(4,128)S(1)} %pad_add_fusion.1), channel_id=1, source_target_pairs={{4,0},{8,4},{12,8},{16,12},{20,16},{24,20},{28,24},{5,1},{9,5},{13... | collective-permute-start | bytes 101384 | tf_op jit(solution)/shard_map/ppermute | solution.py:19
  345.1 14.1 %all-to-all-start.8 = ((f32[32,1,640]{2,1,0:T(1,128)}), f32[32,1,640]{2,1,0:T(1,128)S(1)}, u32[]{:S(2)}, u32[]{:S(2)}) async-start(f32[32,1,640]{2,1,0:T(1,128)} %bitcast.102), calls=%async_computation.8 | async-start | bytes 163840 | tf_op jit(solution)/shard_map/all_to_all | solution.py:54
  360.0 10.9 %all-to-all-start.9 = ((f32[32,1,640]{2,1,0:T(1,128)}), f32[32,1,640]{2,1,0:T(1,128)S(1)}, u32[]{:S(2)}, u32[]{:S(2)}) async-start(f32[32,1,640]{2,1,0:T(1,128)} %stack.20), calls=%async_computation.9 | async-start | bytes 163840 | tf_op jit(solution)/shard_map/all_to_all | solution.py:57
  (60 other events, 305.3 us)
Sparse Core Ops, SparseCore 0:
  49.6 26.9 all-gather.5
  305.1 66.0 all-gather.3
